TPU v7x, 32 devices: a whole 2x2x4 slice. The times are simulated.
32 devices in a mesh: rows: 16 (over z, y, core), cols: 2 (over x).
Axes of the slice: x: 2, y: 2, z: 4, core: 2. Of those that a mesh axis runs over, the one named last changes fastest.
Arguments:
- inputs: bfloat16 [96, 64, 640], P('rows', 'cols'), may hold values from -4 to 4
- qkv_weight: bfloat16 [640, 960], replicated, may hold values from -0.25 to 0.25
- out_weight: bfloat16 [320, 640], replicated, may hold values from -0.3125 to 0.3125
- attn_out: bfloat16 [96, 64, 320], P('rows', 'cols'), may hold values from -6 to 6
- log_norm: float32 [5, 96, 64], P(None, 'rows', 'cols'), may hold values from 4 to 6
- cotangent: bfloat16 [96, 64, 640], P('rows', 'cols'), may hold values from -6 to 6
Outputs:
- grad_input: bfloat16 [96, 64, 640], P('rows', 'cols')
- grad_qkv_weight: bfloat16 [640, 960], replicated
- grad_out_weight: bfloat16 [320, 640], replicated
All inputs are finite; a program needn't handle non-finite values.
Results may differ from a plain program's by a relative error of at most 0.01.
Values may be sent and summed in bfloat16 or wider, within the bound.
A program may use at most 64 MiB of HBM per device.

v0:
```python
import jax
import jax.numpy as jnp
from jax import lax
from jax.sharding import PartitionSpec as P

HEADS = 5
HEAD_DIM = 64
RADIUS = 6


def padded(block, sides, width):
    for axis, dim in sides:
        count = lax.axis_size(axis)
        forward = [(i, i + 1) for i in range(count - 1)]
        forward.append((count - 1, 0))
        backward = [(target, source) for source, target in forward]
        low = lax.ppermute(
            lax.slice_in_dim(block, block.shape[dim] - width, None, axis=dim), axis, forward
        )
        high = lax.ppermute(lax.slice_in_dim(block, 0, width, axis=dim), axis, backward)
        block = jnp.concatenate([low, block, high], axis=dim)
    return block


def window_mask(rows_dev, cols_dev, row_start, grid_rows):
    grown_cols = cols_dev + 2 * RADIUS
    grown_rows = rows_dev + 2 * RADIUS
    own_ids = jnp.arange(rows_dev * cols_dev)
    own_row = own_ids // cols_dev
    own_col = own_ids % cols_dev
    near_ids = jnp.arange(grown_rows * grown_cols)
    near_row = near_ids // grown_cols
    near_col = near_ids % grown_cols
    close_rows = jnp.abs(near_row[None, :] - RADIUS - own_row[:, None]) <= RADIUS
    close_cols = jnp.abs(near_col[None, :] - RADIUS - own_col[:, None]) <= RADIUS
    global_row = row_start + near_row - RADIUS
    in_grid = (global_row >= 0) & (global_row < grid_rows)
    return close_rows & close_cols & in_grid[None, :]


def shards(inputs, qkv_weight, out_weight, attn_out, log_norm, cotangent):
    rows_dev, cols_dev, model_width = inputs.shape
    tokens_dev = rows_dev * cols_dev
    inner_width = HEADS * HEAD_DIM
    score_scale = HEAD_DIM ** (-0.5)
    grown_rows = rows_dev + 2 * RADIUS
    grown_cols = cols_dev + 2 * RADIUS
    grown_tokens = grown_rows * grown_cols
    grid_tokens = tokens_dev * lax.axis_size("rows") * lax.axis_size("cols")
    grad_factor = grid_tokens ** (-0.5)
    flat_in = inputs.reshape(tokens_dev, model_width)
    flat_cot = cotangent.reshape(tokens_dev, model_width)
    flat_att = attn_out.reshape(tokens_dev, inner_width)
    projected = jnp.dot(flat_in, qkv_weight, preferred_element_type=jnp.float32).astype(
        jnp.bfloat16
    )
    grad_att = lax.dot_general(
        flat_cot, out_weight, (((1,), (1,)), ((), ())), preferred_element_type=jnp.float32
    ).astype(jnp.bfloat16)
    grad_wout = lax.dot_general(
        flat_att, flat_cot, (((0,), (0,)), ((), ())), preferred_element_type=jnp.float32
    )
    head_shape = (tokens_dev, HEADS, HEAD_DIM)
    queries = projected[:, :inner_width].reshape(head_shape)
    own_keyval = projected[:, inner_width:]
    upstream = grad_att.reshape(head_shape)
    row_delta = jnp.sum(
        upstream.astype(jnp.float32) * flat_att.reshape(head_shape).astype(jnp.float32), axis=2
    ).T
    own_norm = log_norm.reshape(HEADS, tokens_dev)
    inside = window_mask(
        rows_dev, cols_dev, lax.axis_index("rows") * rows_dev, rows_dev * lax.axis_size("rows")
    )
    block_keyval = own_keyval.reshape(rows_dev, cols_dev, 2 * inner_width)
    query_side = jnp.concatenate([projected[:, :inner_width], grad_att], axis=1).reshape(
        rows_dev, cols_dev, 2 * inner_width
    )
    near_keyval, near_qdo = (
        padded(block_keyval, (("rows", 0), ("cols", 1)), RADIUS),
        padded(query_side, (("rows", 0), ("cols", 1)), RADIUS),
    )
    own_stats = jnp.concatenate([own_norm, row_delta], axis=0).T.reshape(
        rows_dev, cols_dev, 2 * HEADS
    )
    near_stats = padded(own_stats, (("rows", 0), ("cols", 1)), RADIUS)
    flat_kv = near_keyval.reshape(grown_tokens, 2 * inner_width)
    near_keys = flat_kv[:, :inner_width].reshape(grown_tokens, HEADS, HEAD_DIM)
    near_values = flat_kv[:, inner_width:].reshape(grown_tokens, HEADS, HEAD_DIM)
    scores = (
        jnp.einsum("thd,ehd->hte", queries, near_keys, preferred_element_type=jnp.float32)
        * score_scale
    )
    weight = jnp.where(inside[None], jnp.exp(scores - own_norm[:, :, None]), 0.0)
    grad_weight = jnp.einsum(
        "thd,ehd->hte", upstream, near_values, preferred_element_type=jnp.float32
    )
    grad_score = (weight * (grad_weight - row_delta[:, :, None])).astype(jnp.bfloat16)
    grad_query = (
        jnp.einsum("hte,ehd->thd", grad_score, near_keys, preferred_element_type=jnp.float32)
        * score_scale
    )
    near_flat = near_qdo.reshape(grown_tokens, 2 * inner_width)
    near_queries = near_flat[:, :inner_width].reshape(grown_tokens, HEADS, HEAD_DIM)
    near_upstream = near_flat[:, inner_width:].reshape(grown_tokens, HEADS, HEAD_DIM)
    stats_flat = near_stats.reshape(grown_tokens, 2 * HEADS).T
    near_norm = stats_flat[:HEADS]
    near_delta = stats_flat[HEADS:]
    own_keys = own_keyval[:, :inner_width].reshape(head_shape)
    own_values = own_keyval[:, inner_width:].reshape(head_shape)
    scores_back = (
        jnp.einsum("ehd,thd->het", near_queries, own_keys, preferred_element_type=jnp.float32)
        * score_scale
    )
    weight_back = jnp.where(inside.T[None], jnp.exp(scores_back - near_norm[:, :, None]), 0.0)
    grad_back = jnp.einsum(
        "ehd,thd->het", near_upstream, own_values, preferred_element_type=jnp.float32
    )
    score_back_grad = (weight_back * (grad_back - near_delta[:, :, None])).astype(jnp.bfloat16)
    grad_keys = (
        jnp.einsum(
            "het,ehd->thd", score_back_grad, near_queries, preferred_element_type=jnp.float32
        )
        * score_scale
    )
    grad_values = jnp.einsum(
        "het,ehd->thd",
        weight_back.astype(jnp.bfloat16),
        near_upstream,
        preferred_element_type=jnp.float32,
    )
    grad_keyval = jnp.concatenate(
        [grad_keys.reshape(tokens_dev, inner_width), grad_values.reshape(tokens_dev, inner_width)],
        axis=1,
    )
    grad_proj = jnp.concatenate(
        [grad_query.reshape(tokens_dev, inner_width), grad_keyval], axis=1
    ).astype(jnp.bfloat16)
    grad_input = lax.dot_general(
        grad_proj, qkv_weight, (((1,), (1,)), ((), ())), preferred_element_type=jnp.float32
    ).astype(jnp.bfloat16)
    grad_input = grad_input.reshape(rows_dev, cols_dev, model_width)
    grad_wqkv = lax.dot_general(
        flat_in, grad_proj, (((0,), (0,)), ((), ())), preferred_element_type=jnp.float32
    )
    summed_wqkv, summed_wout = lax.psum((grad_wqkv, grad_wout), ("rows", "cols"))
    return (
        grad_input,
        (summed_wqkv * grad_factor).astype(jnp.bfloat16),
        (summed_wout * grad_factor).astype(jnp.bfloat16),
    )


def solution(mesh):
    in_specs = (
        P("rows", "cols", None),
        P(),
        P(),
        P("rows", "cols", None),
        P(None, "rows", "cols"),
        P("rows", "cols", None),
    )
    out_specs = (P("rows", "cols", None), P(), P())
    return jax.shard_map(shards, mesh=mesh, in_specs=in_specs, out_specs=out_specs, check_vma=False)
```

profile of v0, /device:TPU:0, one launch (start us, length us, event | category | flops | bytes accessed | tf_op | source)
XLA Modules:
  0.0 226.1 jit_solution(4671440812148472614)
XLA Ops:
  7.3 1.2 copy-done
  8.5 1.5 convolution_convert_fusion
  10.0 0.8 fusion.37
  10.8 0.3 convolution_convert_fusion.2
  11.2 5.5 %collective-permute-start.5 = (bf16[6,32,640]{2,1,0:T(8,128)(2,1)S(1)}, bf16[6,32,640]{2,1,0:T(8,128)(2,1)S(1)}, u32[]{:S(2)}, u32[]{:S(2)}) collective-permute-start(bf16[6,32,640]{2,1,0:T(8,128)(2,1)S(1)} %bitcast.57), channel_id=1, source_target_pairs={{2,0},{4,2},{6,4},{8,6},{10,8},{12,10},{14,12},{16,14},{18,16},{20... | collective-permute-start | bytes 737288 | tf_op jit(solution)/shard_map/ppermute | solution.py:20
  17.0 0.2 copy.25
  17.3 0.8 sub.133
  18.3 4.4 %collective-permute-start.9 = (f32[6,32,10]{1,0,2:T(8,128)S(1)}, f32[6,32,10]{1,0,2:T(8,128)S(1)}, u32[]{:S(2)}, u32[]{:S(2)}) collective-permute-start(f32[6,32,10]{1,0,2:T(8,128)S(1)} %reshape.285), channel_id=1, source_target_pairs={{2,0},{4,2},{6,4},{8,6},{10,8},{12,10},{14,12},{16,14},{18,16},{20... | collective-permute-start | bytes 23048 | tf_op jit(solution)/shard_map/ppermute | solution.py:20
  22.9 4.5 %collective-permute-start.1 = (bf16[6,32,640]{2,1,0:T(8,128)(2,1)S(1)}, bf16[6,32,640]{2,1,0:T(8,128)(2,1)S(1)}, u32[]{:S(2)}, u32[]{:S(2)}) collective-permute-start(bf16[6,32,640]{2,1,0:T(8,128)(2,1)S(1)} %bitcast.61), channel_id=1, source_target_pairs={{2,0},{4,2},{6,4},{8,6},{10,8},{12,10},{14,12},{16,14},{18,16},{20... | collective-permute-start | bytes 737288 | tf_op jit(solution)/shard_map/ppermute | solution.py:20
  27.4 1.1 fusion.16
  28.5 1.1 fusion.14
  29.7 1.6 collective-permute-start.11
  31.2 0.5 collective-permute-start.10
  31.8 2.2 convolution_bitcast_fusion.1
  34.2 0.8 copy.27
  35.0 0.8 copy.29
  35.8 0.5 collective-permute-done.10
  36.3 1.1 pad_maximum_fusion.13
  37.5 0.9 pad_maximum_fusion.8
  38.4 1.3 collective-permute-start.7
  39.7 0.8 collective-permute-start.6
  40.5 0.6 fusion.39
  41.1 3.0 %collective-permute-done = bf16[6,32,640]{2,1,0:T(8,128)(2,1)S(1)} collective-permute-done((bf16[6,32,640]{2,1,0:T(8,128)(2,1)S(1)}, bf16[6,32,640]{2,1,0:T(8,128)(2,1)S(1)}, u32[]{:S(2)}, u32[]{:S(2)}) %collective-permute-start) | collective-permute-done | bytes 245792 | tf_op jit(solution)/shard_map/ppermute | solution.py:17
  44.1 0.8 pad_maximum_fusion.11
  44.9 1.5 collective-permute-start.3
  46.4 0.5 collective-permute-start.2
  47.0 1.9 collective-permute-done.6
  48.8 1.4 pad_maximum_fusion.1
  50.2 0.2 reshape.282
  50.4 1.1 fusion.36
  51.5 2.2 copy.31
  53.7 1.1 copy.30
  54.8 1.5 pad_maximum_fusion
  56.3 0.2 reshape.274
  56.5 1.1 fusion.35
  57.6 1.4 copy.21
  59.1 1.1 copy.24
  60.2 0.7 fusion.41
  60.8 0.4 copy-done.16
  61.2 1.6 fusion.10
  62.8 4.3 %fusion.9 = bf16[5,64,192]{2,1,0:T(8,128)(2,1)} fusion(bf16[792,5,64]{0,2,1:T(8,128)(2,1)S(1)} %bitcast.54, f32[5,792,192]{1,2,0:T(8,128)} %copy-done.1, bf16[792,5,64]{0,2,1:T(8,128)(2,1)S(1)} %bitcast.72, bf16[192,5,64]{0,2,1:T(8,128)(2,1)S(1)} %bitcast.82, f32[5,792]{1,0:T(8,128)S(1)} %copy-done.26, f32[5,792]{1,0:T(8,128)S(1)} %copy-done.27, ...), kind=kOutput, calls=%fused_computation.16 | convolution fusion | flops 199326720 | bytes 4484544 | tf_op jit(solution)/shard_map/het,ehd->thd/dot_general | solution.py:120
  67.1 2.4 %fusion.40 = f32[5,192,792]{2,1,0:T(8,128)} fusion(bf16[192,5,64]{0,2,1:T(8,128)(2,1)S(1)} %bitcast.67, bf16[792,5,64]{0,2,1:T(8,128)(2,1)S(1)} %bitcast.55), kind=kOutput, calls=%fused_computation.77 | convolution fusion | flops 97320960 | bytes 3671040 | tf_op jit(solution)/shard_map/thd,ehd->hte/dot_general | solution.py:90
  69.5 3.8 %fusion.8 = bf16[5,64,192]{2,1,0:T(8,128)(2,1)S(1)} fusion(bf16[792,5,64]{0,2,1:T(8,128)(2,1)S(1)} %bitcast.56, f32[5,192,792]{2,1,0:T(8,128)} %fusion.40, bf16[192,5,64]{0,2,1:T(8,128)(2,1)S(1)} %bitcast.70, bf16[792,5,64]{0,2,1:T(8,128)(2,1)S(1)} %bitcast.73, f32[5,192]{1,0:T(8,128)S(1)} %bitcast.84, f32[5,192]{1,0:T(8,128)S(1)} %sub.133, ...), kind=kOutput, calls=%fused_computation.15 | convolution fusion | flops 199326720 | bytes 4460544 | tf_op jit(solution)/shard_map/hte,ehd->thd/dot_general | solution.py:99
  73.4 2.0 convolution_bitcast_fusion
  75.4 1.2 convolution_convert_fusion.1
  76.6 138.8 %all-reduce.3.cloned.1.call-done = (f32[640,960]{0,1:T(8,128)}, f32[320,640]{1,0:T(8,128)}) async-done(((f32[640,960]{0,1:T(8,128)}, f32[320,640]{1,0:T(8,128)}), (f32[640,960]{0,1:T(8,128)}, f32[320,640]{1,0:T(8,128)})) %all-reduce.3.cloned.1.call-update) | async-done | bytes 3276816 | tf_op jit(solution)/shard_map/psum | solution.py:145
  215.4 3.0 %multiply_convert_fusion.2 = bf16[640,960]{0,1:T(8,128)(2,1)} fusion(f32[640,960]{0,1:T(8,128)} %get-tuple-element.3), kind=kLoop, calls=%fused_computation.4 | loop fusion | flops 1228800 | bytes 3686400 | tf_op jit(solution)/shard_map/convert_element_type | solution.py:148
  218.4 0.8 multiply_convert_fusion.3
  (82 shorter events, 1.3 us)
Async XLA Ops:
  7.2 1.3 copy-start
  7.2 3.6 %copy-start.19 = (bf16[6,32,640]{2,1,0:T(8,128)(2,1)S(1)}, bf16[6,32,640]{2,1,0:T(8,128)(2,1)}, u32[]{:S(2)}) copy-start(bf16[6,32,640]{2,1,0:T(8,128)(2,1)} %param.11) | copy-start | bytes 737284
  7.2 3.6 %copy-start.18 = (bf16[320,640]{1,0:T(8,128)(2,1)S(1)}, bf16[320,640]{1,0:T(8,128)(2,1)}, u32[]{:S(2)}) copy-start(bf16[320,640]{1,0:T(8,128)(2,1)} %param.8) | copy-start | bytes 1228804
  7.2 9.7 %copy-start.25 = (bf16[6,32,320]{2,1,0:T(8,128)(2,1)S(1)}, bf16[6,32,320]{2,1,0:T(8,128)(2,1)}, u32[]{:S(2)}) copy-start(bf16[6,32,320]{2,1,0:T(8,128)(2,1)} %param.9) | copy-start | bytes 368644
  7.2 208.2 %all-reduce.3.cloned.1.call-start = ((), (), s32[]{:S(2)}) async-start(), calls=%async_computation | async-start | bytes 6553600 | tf_op jit(solution)/shard_map/psum | solution.py:145
  11.2 26.2 %collective-permute-start.5 = (bf16[6,32,640]{2,1,0:T(8,128)(2,1)S(1)}, bf16[6,32,640]{2,1,0:T(8,128)(2,1)S(1)}, u32[]{:S(2)}, u32[]{:S(2)}) collective-permute-start(bf16[6,32,640]{2,1,0:T(8,128)(2,1)S(1)} %bitcast.57), channel_id=1, source_target_pairs={{2,0},{4,2},{6,4},{8,6},{10,8},{12,10},{14,12},{16,14},{18,16},{20... | collective-permute-start | bytes 737288 | tf_op jit(solution)/shard_map/ppermute | solution.py:20
  16.7 20.7 %collective-permute-start.4 = (bf16[6,32,640]{2,1,0:T(8,128)(2,1)S(1)}, bf16[6,32,640]{2,1,0:T(8,128)(2,1)}, u32[]{:S(2)}, u32[]{:S(2)}) collective-permute-start(bf16[6,32,640]{2,1,0:T(8,128)(2,1)S(1)} %bitcast.58), channel_id=1, source_target_pairs={{0,2},{2,4},{4,6},{6,8},{8,10},{10,12},{12,14},{14,16},{16,18},{18... | collective-permute-start | bytes 737288 | tf_op jit(solution)/shard_map/ppermute | solution.py:17
  16.9 14.9 %copy-start.12 = (bf16[192,320]{0,1:T(8,128)(2,1)}, bf16[192,320]{0,1:T(8,128)(2,1)S(1)}, u32[]{:S(2)}) copy-start(bf16[192,320]{0,1:T(8,128)(2,1)S(1)} %copy.23) | copy-start | bytes 368644
  18.1 16.0 %copy-start.15 = (bf16[192,320]{1,0:T(8,128)(2,1)S(1)}, bf16[192,320]{1,0:T(8,128)(2,1)}, u32[]{:S(2)}) copy-start(bf16[192,320]{1,0:T(8,128)(2,1)} %get-tuple-element.14) | copy-start | bytes 368644
  18.2 16.8 %copy-start.14 = (bf16[192,320]{1,0:T(8,128)(2,1)S(1)}, bf16[192,320]{1,0:T(8,128)(2,1)}, u32[]{:S(2)}) copy-start(bf16[192,320]{1,0:T(8,128)(2,1)} %get-tuple-element.13) | copy-start | bytes 368644
  18.3 11.3 %collective-permute-start.9 = (f32[6,32,10]{1,0,2:T(8,128)S(1)}, f32[6,32,10]{1,0,2:T(8,128)S(1)}, u32[]{:S(2)}, u32[]{:S(2)}) collective-permute-start(f32[6,32,10]{1,0,2:T(8,128)S(1)} %reshape.285), channel_id=1, source_target_pairs={{2,0},{4,2},{6,4},{8,6},{10,8},{12,10},{14,12},{16,14},{18,16},{20... | collective-permute-start | bytes 23048 | tf_op jit(solution)/shard_map/ppermute | solution.py:20
  22.7 6.9 %collective-permute-start.8 = (f32[6,32,10]{1,0,2:T(8,128)S(1)}, f32[6,32,10]{1,0,2:T(8,128)S(1)}, u32[]{:S(2)}, u32[]{:S(2)}) collective-permute-start(f32[6,32,10]{1,0,2:T(8,128)S(1)} %reshape.285), channel_id=1, source_target_pairs={{0,2},{2,4},{4,6},{6,8},{8,10},{10,12},{12,14},{14,16},{16,18},{18... | collective-permute-start | bytes 23048 | tf_op jit(solution)/shard_map/ppermute | solution.py:17
  22.8 21.3 %copy-start.3 = (bf16[192,640]{1,0:T(8,128)(2,1)}, bf16[192,640]{1,0:T(8,128)(2,1)S(1)}, u32[]{:S(2)}) copy-start(bf16[192,640]{1,0:T(8,128)(2,1)S(1)} %slice.67) | copy-start | bytes 737284
  22.9 18.2 %collective-permute-start.1 = (bf16[6,32,640]{2,1,0:T(8,128)(2,1)S(1)}, bf16[6,32,640]{2,1,0:T(8,128)(2,1)S(1)}, u32[]{:S(2)}, u32[]{:S(2)}) collective-permute-start(bf16[6,32,640]{2,1,0:T(8,128)(2,1)S(1)} %bitcast.61), channel_id=1, source_target_pairs={{2,0},{4,2},{6,4},{8,6},{10,8},{12,10},{14,12},{16,14},{18,16},{20... | collective-permute-start | bytes 737288 | tf_op jit(solution)/shard_map/ppermute | solution.py:20
  29.7 6.1 %collective-permute-start.11 = (f32[18,6,10]{1,0,2:T(8,128)S(1)}, f32[18,6,10]{1,0,2:T(8,128)S(1)}, u32[]{:S(2)}, u32[]{:S(2)}) collective-permute-start(f32[18,6,10]{1,0,2:T(8,128)S(1)} %get-tuple-element.17), channel_id=1, source_target_pairs={{1,0},{0,1},{3,2},{2,3},{5,4},{4,5},{7,6},{6,7},{9,8},{8,9},{11,10... | collective-permute-start | bytes 12968 | tf_op jit(solution)/shard_map/ppermute | solution.py:20
  31.2 5.0 %collective-permute-start.10 = (f32[18,6,10]{1,0,2:T(8,128)S(1)}, f32[18,6,10]{1,0,2:T(8,128)}, u32[]{:S(2)}, u32[]{:S(2)}) collective-permute-start(f32[18,6,10]{1,0,2:T(8,128)S(1)} %get-tuple-element.16), channel_id=1, source_target_pairs={{0,1},{1,0},{2,3},{3,2},{4,5},{5,4},{6,7},{7,6},{8,9},{9,8},{10,11... | collective-permute-start | bytes 12968 | tf_op jit(solution)/shard_map/ppermute | solution.py:17
  35.8 8.3 %collective-permute-start = (bf16[6,32,640]{2,1,0:T(8,128)(2,1)S(1)}, bf16[6,32,640]{2,1,0:T(8,128)(2,1)S(1)}, u32[]{:S(2)}, u32[]{:S(2)}) collective-permute-start(bf16[6,32,640]{2,1,0:T(8,128)(2,1)S(1)} %bitcast.62), channel_id=1, source_target_pairs={{0,2},{2,4},{4,6},{6,8},{8,10},{10,12},{12,14},{14,16},{16,18},{18... | collective-permute-start | bytes 737288 | tf_op jit(solution)/shard_map/ppermute | solution.py:17
  38.4 8.6 %collective-permute-start.7 = (bf16[18,6,640]{2,1,0:T(8,128)(2,1)S(1)}, bf16[18,6,640]{2,1,0:T(8,128)(2,1)S(1)}, u32[]{:S(2)}, u32[]{:S(2)}) collective-permute-start(bf16[18,6,640]{2,1,0:T(8,128)(2,1)S(1)} %get-tuple-element.12), channel_id=1, source_target_pairs={{1,0},{0,1},{3,2},{2,3},{5,4},{4,5},{7,6},{6,7},{9,8},{8,9},{11,10... | collective-permute-start | bytes 414728 | tf_op jit(solution)/shard_map/ppermute | solution.py:20
  39.7 9.1 %collective-permute-start.6 = (bf16[18,6,640]{2,1,0:T(8,128)(2,1)S(1)}, bf16[18,6,640]{2,1,0:T(8,128)(2,1)S(1)}, u32[]{:S(2)}, u32[]{:S(2)}) collective-permute-start(bf16[18,6,640]{2,1,0:T(8,128)(2,1)S(1)} %get-tuple-element.11), channel_id=1, source_target_pairs={{0,1},{1,0},{2,3},{3,2},{4,5},{5,4},{6,7},{7,6},{8,9},{9,8},{10,11... | collective-permute-start | bytes 414728 | tf_op jit(solution)/shard_map/ppermute | solution.py:17
  41.1 7.7 %copy-start.6 = (bf16[6,32,640]{2,1,0:T(8,128)(2,1)}, bf16[6,32,640]{2,1,0:T(8,128)(2,1)S(1)}, u32[]{:S(2)}) copy-start(bf16[6,32,640]{2,1,0:T(8,128)(2,1)S(1)} %collective-permute-done.1) | copy-start | bytes 737284
  44.1 2.9 %copy-start.8 = (bf16[6,32,640]{2,1,0:T(8,128)(2,1)}, bf16[6,32,640]{2,1,0:T(8,128)(2,1)S(1)}, u32[]{:S(2)}) copy-start(bf16[6,32,640]{2,1,0:T(8,128)(2,1)S(1)} %collective-permute-done) | copy-start | bytes 737284
  44.9 9.9 %collective-permute-start.3 = (bf16[18,6,640]{2,1,0:T(8,128)(2,1)}, bf16[18,6,640]{2,1,0:T(8,128)(2,1)}, u32[]{:S(2)}, u32[]{:S(2)}) collective-permute-start(bf16[18,6,640]{2,1,0:T(8,128)(2,1)} %get-tuple-element.10), channel_id=1, source_target_pairs={{1,0},{0,1},{3,2},{2,3},{5,4},{4,5},{7,6},{6,7},{9,8},{8,9},{11,10... | collective-permute-start | bytes 414728 | tf_op jit(solution)/shard_map/ppermute | solution.py:20
  46.4 8.4 %collective-permute-start.2 = (bf16[18,6,640]{2,1,0:T(8,128)(2,1)}, bf16[18,6,640]{2,1,0:T(8,128)(2,1)}, u32[]{:S(2)}, u32[]{:S(2)}) collective-permute-start(bf16[18,6,640]{2,1,0:T(8,128)(2,1)} %get-tuple-element.9), channel_id=1, source_target_pairs={{0,1},{1,0},{2,3},{3,2},{4,5},{5,4},{6,7},{7,6},{8,9},{9,8},{10,11... | collective-permute-start | bytes 414728 | tf_op jit(solution)/shard_map/ppermute | solution.py:17
  51.5 3.3 %copy-start.4 = (bf16[192,640]{1,0:T(8,128)(2,1)S(1)}, bf16[192,640]{1,0:T(8,128)(2,1)}, u32[]{:S(2)}) copy-start(bf16[192,640]{1,0:T(8,128)(2,1)} %copy-done.3) | copy-start | bytes 737284
  51.5 3.3 %copy-start.7 = (bf16[6,32,640]{2,1,0:T(8,128)(2,1)S(1)}, bf16[6,32,640]{2,1,0:T(8,128)(2,1)}, u32[]{:S(2)}) copy-start(bf16[6,32,640]{2,1,0:T(8,128)(2,1)} %copy-done.6) | copy-start | bytes 737284
  51.5 3.3 %copy-start.9 = (bf16[6,32,640]{2,1,0:T(8,128)(2,1)S(1)}, bf16[6,32,640]{2,1,0:T(8,128)(2,1)}, u32[]{:S(2)}) copy-start(bf16[6,32,640]{2,1,0:T(8,128)(2,1)} %copy-done.8) | copy-start | bytes 737284
  57.6 2.5 %copy-start.2 = (bf16[792,320]{0,1:T(8,128)(2,1)S(1)}, bf16[792,320]{0,1:T(8,128)(2,1)}, u32[]{:S(2)}) copy-start(bf16[792,320]{0,1:T(8,128)(2,1)} %copy.30) | copy-start | bytes 1520644
  57.6 2.5 %copy-start.11 = (bf16[192,320]{0,1:T(8,128)(2,1)S(1)}, bf16[192,320]{0,1:T(8,128)(2,1)}, u32[]{:S(2)}) copy-start(bf16[192,320]{0,1:T(8,128)(2,1)} %copy.27) | copy-start | bytes 368644
  60.1 1.1 copy-start.16
  60.1 1.1 copy-start.21
  60.1 1.1 copy-start.27
  60.8 2.0 copy-start.1
  61.2 1.6 copy-start.24
  61.2 1.6 copy-start.26
  67.1 2.4 %copy-start.13 = (bf16[192,320]{0,1:T(8,128)(2,1)S(1)}, bf16[192,320]{0,1:T(8,128)(2,1)}, u32[]{:S(2)}) copy-start(bf16[192,320]{0,1:T(8,128)(2,1)} %copy-done.12) | copy-start | bytes 368644
  67.1 2.4 %copy-start.17 = (bf16[792,320]{0,1:T(8,128)(2,1)S(1)}, bf16[792,320]{0,1:T(8,128)(2,1)}, u32[]{:S(2)}) copy-start(bf16[792,320]{0,1:T(8,128)(2,1)} %copy.24) | copy-start | bytes 1520644
  67.1 2.4 %copy-start.20 = (pred[192,792]{1,0:T(8,128)(4,1)S(1)}, pred[192,792]{1,0:T(8,128)(4,1)}, u32[]{:S(2)}) copy-start(pred[192,792]{1,0:T(8,128)(4,1)} %fusion.14) | copy-start | bytes 456196
  69.5 3.8 %copy-start.5 = (bf16[6,32,640]{2,1,0:T(8,128)(2,1)S(1)}, bf16[6,32,640]{2,1,0:T(8,128)(2,1)}, u32[]{:S(2)}) copy-start(bf16[6,32,640]{2,1,0:T(8,128)(2,1)} %param.6) | copy-start | bytes 737284
  69.5 3.8 %copy-start.22 = (bf16[5,64,192]{2,1,0:T(8,128)(2,1)S(1)}, bf16[5,64,192]{2,1,0:T(8,128)(2,1)}, u32[]{:S(2)}) copy-start(bf16[5,64,192]{2,1,0:T(8,128)(2,1)} %fusion.10) | copy-start | bytes 368644
  69.5 3.8 %copy-start.23 = (bf16[5,64,192]{2,1,0:T(8,128)(2,1)S(1)}, bf16[5,64,192]{2,1,0:T(8,128)(2,1)}, u32[]{:S(2)}) copy-start(bf16[5,64,192]{2,1,0:T(8,128)(2,1)} %fusion.9) | copy-start | bytes 368644
  215.4 3.0 %copy-start.10 = (f32[320,640]{1,0:T(8,128)S(1)}, f32[320,640]{1,0:T(8,128)}, u32[]{:S(2)}) copy-start(f32[320,640]{1,0:T(8,128)} %get-tuple-element.4) | copy-start | bytes 2457604
Sparse Core Ops, SparseCore 0:
  75.6 139.7 all-reduce.2
where the time goes:
time: 227 us; the launch traced here: 226 us
  waiting for transfers between devices  144 us (63%)
  starting transfers between devices  20.7 us (9%)
  matrix products  20 us (9%)
  local copies, waits for them, and re-layouts  14.9 us (7%)
  between operations  14.4 us (6%)
  other arithmetic  11.9 us (5%)
    psum x1, waiting for transfers between devices, shards(): lax.psum((grad_wqkv, grad_wout), ('rows', 'cols'))  139 us
    ppermute x6, starting transfers between devices, padded(): lax.ppermute(lax.slice_in_dim(block, 0, width, axis=dim), axis, backward)  18.8 us
    ppermute x6, waiting for transfers between devices, padded(): lax.ppermute(lax.slice_in_dim(block, block.shape[dim] - width, None, axis...  5.37 us
    unnamed x58, local copies, waits for them, and re-layouts  5.03 us
  transfers between devices with their start and end apart: 13, of which 4 were waited for; matrix products, arithmetic and copies ran while one was open for 8% of the time, Pallas kernels for 0%

commit v1 on v0

--- a/solution.py
+++ b/solution.py
@@ -142,7 +142,7 @@
     grad_wqkv = lax.dot_general(
         flat_in, grad_proj, (((0,), (0,)), ((), ())), preferred_element_type=jnp.float32
     )
-    summed_wqkv, summed_wout = lax.psum((grad_wqkv, grad_wout), ("rows", "cols"))
+    summed_wqkv, summed_wout = lax.psum(lax.psum((grad_wqkv, grad_wout), "cols"), "rows")
     return (
         grad_input,
         (summed_wqkv * grad_factor).astype(jnp.bfloat16),

time: 227 us -> 285 us (1.26)
  waiting for transfers between devices: 144 us -> 202 us
    psum x1 -> x2, waiting for transfers between devices: 139 us -> 197 us  [the longest x1 107 us: shards(): lax.psum(lax.psum((grad_wqkv, grad_wout), 'cols'), 'rows')]
  transfers between devices with their start and end apart: 13 -> 14, of which waited for: 4 -> 5; matrix products, arithmetic and copies ran while one was open for 8% -> 7% of each run, Pallas kernels for 0% -> 0%
where the time goes in v1:
time: 285 us; the launch traced here: 284 us
  waiting for transfers between devices  202 us (71%)
  starting transfers between devices  20.8 us (7%)
  matrix products  20 us (7%)
  local copies, waits for them, and re-layouts  15 us (5%)
  between operations  14.4 us (5%)
  other arithmetic  11.9 us (4%)
    psum x1, waiting for transfers between devices, shards(): lax.psum(lax.psum((grad_wqkv, grad_wout), 'cols'), 'rows')  107 us
    psum x1, waiting for transfers between devices, shards(): lax.psum((grad_wqkv, grad_wout), 'cols')  89.7 us
    ppermute x6, starting transfers between devices, padded(): lax.ppermute(lax.slice_in_dim(block, 0, width, axis=dim), axis, backward)  18.8 us
  transfers between devices with their start and end apart: 14, of which 5 were waited for; matrix products, arithmetic and copies ran while one was open for 7% of the time, Pallas kernels for 0%

profile of v1, /device:TPU:0, one launch (start us, length us, event | category | flops | bytes accessed | tf_op | source)
XLA Modules:
  0.0 284.1 jit_solution(11987115370980488941)
XLA Ops:
  7.3 1.2 copy-done
  8.5 1.5 convolution_convert_fusion
  10.0 0.8 fusion.37
  10.7 0.3 convolution_convert_fusion.2
  11.2 5.5 %collective-permute-start.5 = (bf16[6,32,640]{2,1,0:T(8,128)(2,1)S(1)}, bf16[6,32,640]{2,1,0:T(8,128)(2,1)S(1)}, u32[]{:S(2)}, u32[]{:S(2)}) collective-permute-start(bf16[6,32,640]{2,1,0:T(8,128)(2,1)S(1)} %bitcast.57), channel_id=1, source_target_pairs={{2,0},{4,2},{6,4},{8,6},{10,8},{12,10},{14,12},{16,14},{18,16},{20... | collective-permute-start | bytes 737288 | tf_op jit(solution)/shard_map/ppermute | solution.py:20
  17.0 0.2 copy.25
  17.3 0.8 sub.133
  18.2 4.4 %collective-permute-start.9 = (f32[6,32,10]{1,0,2:T(8,128)S(1)}, f32[6,32,10]{1,0,2:T(8,128)S(1)}, u32[]{:S(2)}, u32[]{:S(2)}) collective-permute-start(f32[6,32,10]{1,0,2:T(8,128)S(1)} %reshape.285), channel_id=1, source_target_pairs={{2,0},{4,2},{6,4},{8,6},{10,8},{12,10},{14,12},{16,14},{18,16},{20... | collective-permute-start | bytes 23048 | tf_op jit(solution)/shard_map/ppermute | solution.py:20
  22.8 4.5 %collective-permute-start.1 = (bf16[6,32,640]{2,1,0:T(8,128)(2,1)S(1)}, bf16[6,32,640]{2,1,0:T(8,128)(2,1)S(1)}, u32[]{:S(2)}, u32[]{:S(2)}) collective-permute-start(bf16[6,32,640]{2,1,0:T(8,128)(2,1)S(1)} %bitcast.61), channel_id=1, source_target_pairs={{2,0},{4,2},{6,4},{8,6},{10,8},{12,10},{14,12},{16,14},{18,16},{20... | collective-permute-start | bytes 737288 | tf_op jit(solution)/shard_map/ppermute | solution.py:20
  27.4 1.1 fusion.16
  28.4 1.1 fusion.14
  29.7 1.6 collective-permute-start.11
  31.2 0.5 collective-permute-start.10
  31.8 2.2 convolution_bitcast_fusion.1
  34.1 0.8 copy.27
  34.9 0.8 copy.29
  35.7 0.5 collective-permute-done.10
  36.3 1.1 pad_maximum_fusion.13
  37.5 0.9 pad_maximum_fusion.8
  38.4 1.3 collective-permute-start.7
  39.7 0.8 collective-permute-start.6
  40.5 0.6 fusion.39
  41.1 3.0 %collective-permute-done = bf16[6,32,640]{2,1,0:T(8,128)(2,1)S(1)} collective-permute-done((bf16[6,32,640]{2,1,0:T(8,128)(2,1)S(1)}, bf16[6,32,640]{2,1,0:T(8,128)(2,1)S(1)}, u32[]{:S(2)}, u32[]{:S(2)}) %collective-permute-start) | collective-permute-done | bytes 245792 | tf_op jit(solution)/shard_map/ppermute | solution.py:17
  44.1 0.8 pad_maximum_fusion.11
  44.9 1.5 collective-permute-start.3
  46.4 0.5 collective-permute-start.2
  46.9 1.9 collective-permute-done.6
  48.8 1.4 pad_maximum_fusion.1
  50.2 0.2 reshape.282
  50.4 1.1 fusion.36
  51.5 2.2 copy.31
  53.7 1.1 copy.30
  54.8 1.5 pad_maximum_fusion
  56.5 1.1 fusion.35
  57.6 1.4 copy.21
  59.0 1.1 copy.24
  60.2 0.7 fusion.41
  60.8 0.4 copy-done.16
  61.2 1.6 fusion.10
  62.8 4.3 %fusion.9 = bf16[5,64,192]{2,1,0:T(8,128)(2,1)} fusion(bf16[792,5,64]{0,2,1:T(8,128)(2,1)S(1)} %bitcast.54, f32[5,792,192]{1,2,0:T(8,128)} %copy-done.1, bf16[792,5,64]{0,2,1:T(8,128)(2,1)S(1)} %bitcast.72, bf16[192,5,64]{0,2,1:T(8,128)(2,1)S(1)} %bitcast.82, f32[5,792]{1,0:T(8,128)S(1)} %copy-done.26, f32[5,792]{1,0:T(8,128)S(1)} %copy-done.27, ...), kind=kOutput, calls=%fused_computation.16 | convolution fusion | flops 199326720 | bytes 4484544 | tf_op jit(solution)/shard_map/het,ehd->thd/dot_general | solution.py:120
  67.1 2.4 fusion.40
  69.5 3.8 %fusion.8 = bf16[5,64,192]{2,1,0:T(8,128)(2,1)S(1)} fusion(bf16[792,5,64]{0,2,1:T(8,128)(2,1)S(1)} %bitcast.56, f32[5,192,792]{2,1,0:T(8,128)} %fusion.40, bf16[192,5,64]{0,2,1:T(8,128)(2,1)S(1)} %bitcast.70, bf16[792,5,64]{0,2,1:T(8,128)(2,1)S(1)} %bitcast.73, f32[5,192]{1,0:T(8,128)S(1)} %bitcast.84, f32[5,192]{1,0:T(8,128)S(1)} %sub.133, ...), kind=kOutput, calls=%fused_computation.15 | convolution fusion | flops 199326720 | bytes 4460544 | tf_op jit(solution)/shard_map/hte,ehd->thd/dot_general | solution.py:99
  73.4 2.0 convolution_bitcast_fusion
  75.5 89.7 %all-reduce.7.cloned.1.call-done = (f32[640,960]{0,1:T(8,128)}, f32[320,640]{1,0:T(8,128)}) async-done(((f32[640,960]{0,1:T(8,128)}, f32[320,640]{1,0:T(8,128)}), (f32[640,960]{0,1:T(8,128)}, f32[320,640]{1,0:T(8,128)})) %all-reduce.7.cloned.1.call-update) | async-done | bytes 3276816 | tf_op jit(solution)/shard_map/psum | solution.py:145
  165.2 1.2 convolution_convert_fusion.1
  166.4 107.0 %all-reduce.5.cloned.1.call-done = (f32[640,960]{0,1:T(8,128)}, f32[320,640]{1,0:T(8,128)}) async-done(((f32[640,960]{0,1:T(8,128)}, f32[320,640]{1,0:T(8,128)}), (f32[640,960]{0,1:T(8,128)}, f32[320,640]{1,0:T(8,128)})) %all-reduce.5.cloned.1.call-update) | async-done | bytes 3276816 | tf_op jit(solution)/shard_map/psum | solution.py:145
  273.4 3.0 %multiply_convert_fusion.2 = bf16[640,960]{0,1:T(8,128)(2,1)} fusion(f32[640,960]{0,1:T(8,128)} %get-tuple-element.3), kind=kLoop, calls=%fused_computation.4 | loop fusion | flops 1228800 | bytes 3686400 | tf_op jit(solution)/shard_map/convert_element_type | solution.py:148
  276.5 0.8 multiply_convert_fusion.3
  (85 shorter events, 1.5 us)
Async XLA Ops:
  7.2 1.3 copy-start
  7.2 3.6 %copy-start.19 = (bf16[6,32,640]{2,1,0:T(8,128)(2,1)S(1)}, bf16[6,32,640]{2,1,0:T(8,128)(2,1)}, u32[]{:S(2)}) copy-start(bf16[6,32,640]{2,1,0:T(8,128)(2,1)} %param.11) | copy-start | bytes 737284
  7.2 3.5 %copy-start.18 = (bf16[320,640]{1,0:T(8,128)(2,1)S(1)}, bf16[320,640]{1,0:T(8,128)(2,1)}, u32[]{:S(2)}) copy-start(bf16[320,640]{1,0:T(8,128)(2,1)} %param.8) | copy-start | bytes 1228804
  7.2 9.6 %copy-start.25 = (bf16[6,32,320]{2,1,0:T(8,128)(2,1)S(1)}, bf16[6,32,320]{2,1,0:T(8,128)(2,1)}, u32[]{:S(2)}) copy-start(bf16[6,32,320]{2,1,0:T(8,128)(2,1)} %param.9) | copy-start | bytes 368644
  7.2 157.9 %all-reduce.7.cloned.1.call-start = ((), (), s32[]{:S(2)}) async-start(), calls=%async_computation.1 | async-start | bytes 6553600 | tf_op jit(solution)/shard_map/psum | solution.py:145
  11.2 26.3 %collective-permute-start.5 = (bf16[6,32,640]{2,1,0:T(8,128)(2,1)S(1)}, bf16[6,32,640]{2,1,0:T(8,128)(2,1)S(1)}, u32[]{:S(2)}, u32[]{:S(2)}) collective-permute-start(bf16[6,32,640]{2,1,0:T(8,128)(2,1)S(1)} %bitcast.57), channel_id=1, source_target_pairs={{2,0},{4,2},{6,4},{8,6},{10,8},{12,10},{14,12},{16,14},{18,16},{20... | collective-permute-start | bytes 737288 | tf_op jit(solution)/shard_map/ppermute | solution.py:20
  16.7 20.7 %collective-permute-start.4 = (bf16[6,32,640]{2,1,0:T(8,128)(2,1)S(1)}, bf16[6,32,640]{2,1,0:T(8,128)(2,1)}, u32[]{:S(2)}, u32[]{:S(2)}) collective-permute-start(bf16[6,32,640]{2,1,0:T(8,128)(2,1)S(1)} %bitcast.58), channel_id=1, source_target_pairs={{0,2},{2,4},{4,6},{6,8},{8,10},{10,12},{12,14},{14,16},{16,18},{18... | collective-permute-start | bytes 737288 | tf_op jit(solution)/shard_map/ppermute | solution.py:17
  16.9 14.9 %copy-start.12 = (bf16[192,320]{0,1:T(8,128)(2,1)}, bf16[192,320]{0,1:T(8,128)(2,1)S(1)}, u32[]{:S(2)}) copy-start(bf16[192,320]{0,1:T(8,128)(2,1)S(1)} %copy.23) | copy-start | bytes 368644
  18.1 16.0 %copy-start.15 = (bf16[192,320]{1,0:T(8,128)(2,1)S(1)}, bf16[192,320]{1,0:T(8,128)(2,1)}, u32[]{:S(2)}) copy-start(bf16[192,320]{1,0:T(8,128)(2,1)} %get-tuple-element.16) | copy-start | bytes 368644
  18.1 16.8 %copy-start.14 = (bf16[192,320]{1,0:T(8,128)(2,1)S(1)}, bf16[192,320]{1,0:T(8,128)(2,1)}, u32[]{:S(2)}) copy-start(bf16[192,320]{1,0:T(8,128)(2,1)} %get-tuple-element.15) | copy-start | bytes 368644
  18.2 11.3 %collective-permute-start.9 = (f32[6,32,10]{1,0,2:T(8,128)S(1)}, f32[6,32,10]{1,0,2:T(8,128)S(1)}, u32[]{:S(2)}, u32[]{:S(2)}) collective-permute-start(f32[6,32,10]{1,0,2:T(8,128)S(1)} %reshape.285), channel_id=1, source_target_pairs={{2,0},{4,2},{6,4},{8,6},{10,8},{12,10},{14,12},{16,14},{18,16},{20... | collective-permute-start | bytes 23048 | tf_op jit(solution)/shard_map/ppermute | solution.py:20
  22.7 6.8 %collective-permute-start.8 = (f32[6,32,10]{1,0,2:T(8,128)S(1)}, f32[6,32,10]{1,0,2:T(8,128)S(1)}, u32[]{:S(2)}, u32[]{:S(2)}) collective-permute-start(f32[6,32,10]{1,0,2:T(8,128)S(1)} %reshape.285), channel_id=1, source_target_pairs={{0,2},{2,4},{4,6},{6,8},{8,10},{10,12},{12,14},{14,16},{16,18},{18... | collective-permute-start | bytes 23048 | tf_op jit(solution)/shard_map/ppermute | solution.py:17
  22.8 21.2 %copy-start.3 = (bf16[192,640]{1,0:T(8,128)(2,1)}, bf16[192,640]{1,0:T(8,128)(2,1)S(1)}, u32[]{:S(2)}) copy-start(bf16[192,640]{1,0:T(8,128)(2,1)S(1)} %slice.67) | copy-start | bytes 737284
  22.8 18.3 %collective-permute-start.1 = (bf16[6,32,640]{2,1,0:T(8,128)(2,1)S(1)}, bf16[6,32,640]{2,1,0:T(8,128)(2,1)S(1)}, u32[]{:S(2)}, u32[]{:S(2)}) collective-permute-start(bf16[6,32,640]{2,1,0:T(8,128)(2,1)S(1)} %bitcast.61), channel_id=1, source_target_pairs={{2,0},{4,2},{6,4},{8,6},{10,8},{12,10},{14,12},{16,14},{18,16},{20... | collective-permute-start | bytes 737288 | tf_op jit(solution)/shard_map/ppermute | solution.py:20
  29.7 6.1 %collective-permute-start.11 = (f32[18,6,10]{1,0,2:T(8,128)S(1)}, f32[18,6,10]{1,0,2:T(8,128)S(1)}, u32[]{:S(2)}, u32[]{:S(2)}) collective-permute-start(f32[18,6,10]{1,0,2:T(8,128)S(1)} %get-tuple-element.19), channel_id=1, source_target_pairs={{1,0},{0,1},{3,2},{2,3},{5,4},{4,5},{7,6},{6,7},{9,8},{8,9},{11,10... | collective-permute-start | bytes 12968 | tf_op jit(solution)/shard_map/ppermute | solution.py:20
  31.2 5.1 %collective-permute-start.10 = (f32[18,6,10]{1,0,2:T(8,128)S(1)}, f32[18,6,10]{1,0,2:T(8,128)}, u32[]{:S(2)}, u32[]{:S(2)}) collective-permute-start(f32[18,6,10]{1,0,2:T(8,128)S(1)} %get-tuple-element.18), channel_id=1, source_target_pairs={{0,1},{1,0},{2,3},{3,2},{4,5},{5,4},{6,7},{7,6},{8,9},{9,8},{10,11... | collective-permute-start | bytes 12968 | tf_op jit(solution)/shard_map/ppermute | solution.py:17
  35.7 8.3 %collective-permute-start = (bf16[6,32,640]{2,1,0:T(8,128)(2,1)S(1)}, bf16[6,32,640]{2,1,0:T(8,128)(2,1)S(1)}, u32[]{:S(2)}, u32[]{:S(2)}) collective-permute-start(bf16[6,32,640]{2,1,0:T(8,128)(2,1)S(1)} %bitcast.62), channel_id=1, source_target_pairs={{0,2},{2,4},{4,6},{6,8},{8,10},{10,12},{12,14},{14,16},{16,18},{18... | collective-permute-start | bytes 737288 | tf_op jit(solution)/shard_map/ppermute | solution.py:17
  38.4 8.6 %collective-permute-start.7 = (bf16[18,6,640]{2,1,0:T(8,128)(2,1)S(1)}, bf16[18,6,640]{2,1,0:T(8,128)(2,1)S(1)}, u32[]{:S(2)}, u32[]{:S(2)}) collective-permute-start(bf16[18,6,640]{2,1,0:T(8,128)(2,1)S(1)} %get-tuple-element.14), channel_id=1, source_target_pairs={{1,0},{0,1},{3,2},{2,3},{5,4},{4,5},{7,6},{6,7},{9,8},{8,9},{11,10... | collective-permute-start | bytes 414728 | tf_op jit(solution)/shard_map/ppermute | solution.py:20
  39.7 9.1 %collective-permute-start.6 = (bf16[18,6,640]{2,1,0:T(8,128)(2,1)S(1)}, bf16[18,6,640]{2,1,0:T(8,128)(2,1)S(1)}, u32[]{:S(2)}, u32[]{:S(2)}) collective-permute-start(bf16[18,6,640]{2,1,0:T(8,128)(2,1)S(1)} %get-tuple-element.13), channel_id=1, source_target_pairs={{0,1},{1,0},{2,3},{3,2},{4,5},{5,4},{6,7},{7,6},{8,9},{9,8},{10,11... | collective-permute-start | bytes 414728 | tf_op jit(solution)/shard_map/ppermute | solution.py:17
  41.1 7.7 %copy-start.6 = (bf16[6,32,640]{2,1,0:T(8,128)(2,1)}, bf16[6,32,640]{2,1,0:T(8,128)(2,1)S(1)}, u32[]{:S(2)}) copy-start(bf16[6,32,640]{2,1,0:T(8,128)(2,1)S(1)} %collective-permute-done.1) | copy-start | bytes 737284
  44.1 2.9 %copy-start.8 = (bf16[6,32,640]{2,1,0:T(8,128)(2,1)}, bf16[6,32,640]{2,1,0:T(8,128)(2,1)S(1)}, u32[]{:S(2)}) copy-start(bf16[6,32,640]{2,1,0:T(8,128)(2,1)S(1)} %collective-permute-done) | copy-start | bytes 737284
  44.9 9.9 %collective-permute-start.3 = (bf16[18,6,640]{2,1,0:T(8,128)(2,1)}, bf16[18,6,640]{2,1,0:T(8,128)(2,1)}, u32[]{:S(2)}, u32[]{:S(2)}) collective-permute-start(bf16[18,6,640]{2,1,0:T(8,128)(2,1)} %get-tuple-element.12), channel_id=1, source_target_pairs={{1,0},{0,1},{3,2},{2,3},{5,4},{4,5},{7,6},{6,7},{9,8},{8,9},{11,10... | collective-permute-start | bytes 414728 | tf_op jit(solution)/shard_map/ppermute | solution.py:20
  46.4 8.4 %collective-permute-start.2 = (bf16[18,6,640]{2,1,0:T(8,128)(2,1)}, bf16[18,6,640]{2,1,0:T(8,128)(2,1)}, u32[]{:S(2)}, u32[]{:S(2)}) collective-permute-start(bf16[18,6,640]{2,1,0:T(8,128)(2,1)} %get-tuple-element.11), channel_id=1, source_target_pairs={{0,1},{1,0},{2,3},{3,2},{4,5},{5,4},{6,7},{7,6},{8,9},{9,8},{10,11... | collective-permute-start | bytes 414728 | tf_op jit(solution)/shard_map/ppermute | solution.py:17
  51.5 3.3 %copy-start.4 = (bf16[192,640]{1,0:T(8,128)(2,1)S(1)}, bf16[192,640]{1,0:T(8,128)(2,1)}, u32[]{:S(2)}) copy-start(bf16[192,640]{1,0:T(8,128)(2,1)} %copy-done.3) | copy-start | bytes 737284
  51.5 3.3 %copy-start.7 = (bf16[6,32,640]{2,1,0:T(8,128)(2,1)S(1)}, bf16[6,32,640]{2,1,0:T(8,128)(2,1)}, u32[]{:S(2)}) copy-start(bf16[6,32,640]{2,1,0:T(8,128)(2,1)} %copy-done.6) | copy-start | bytes 737284
  51.5 3.3 %copy-start.9 = (bf16[6,32,640]{2,1,0:T(8,128)(2,1)S(1)}, bf16[6,32,640]{2,1,0:T(8,128)(2,1)}, u32[]{:S(2)}) copy-start(bf16[6,32,640]{2,1,0:T(8,128)(2,1)} %copy-done.8) | copy-start | bytes 737284
  57.6 2.5 copy-start.2
  57.6 2.5 copy-start.11
  60.1 1.1 copy-start.16
  60.1 1.1 copy-start.21
  60.1 1.1 copy-start.27
  60.8 2.0 copy-start.1
  61.2 1.6 copy-start.24
  61.2 1.6 copy-start.26
  67.1 2.4 copy-start.13
  67.1 2.4 copy-start.17
  67.1 2.4 copy-start.20
  69.5 3.8 %copy-start.5 = (bf16[6,32,640]{2,1,0:T(8,128)(2,1)S(1)}, bf16[6,32,640]{2,1,0:T(8,128)(2,1)}, u32[]{:S(2)}) copy-start(bf16[6,32,640]{2,1,0:T(8,128)(2,1)} %param.6) | copy-start | bytes 737284
  69.5 3.8 %copy-start.22 = (bf16[5,64,192]{2,1,0:T(8,128)(2,1)S(1)}, bf16[5,64,192]{2,1,0:T(8,128)(2,1)}, u32[]{:S(2)}) copy-start(bf16[5,64,192]{2,1,0:T(8,128)(2,1)} %fusion.10) | copy-start | bytes 368644
  69.5 3.8 %copy-start.23 = (bf16[5,64,192]{2,1,0:T(8,128)(2,1)S(1)}, bf16[5,64,192]{2,1,0:T(8,128)(2,1)}, u32[]{:S(2)}) copy-start(bf16[5,64,192]{2,1,0:T(8,128)(2,1)} %fusion.9) | copy-start | bytes 368644
  75.4 198.0 %all-reduce.5.cloned.1.call-start = ((), (), s32[]{:S(2)}) async-start(), calls=%async_computation | async-start | bytes 6553600 | tf_op jit(solution)/shard_map/psum | solution.py:145
  273.4 3.0 %copy-start.10 = (f32[320,640]{1,0:T(8,128)S(1)}, f32[320,640]{1,0:T(8,128)}, u32[]{:S(2)}) copy-start(f32[320,640]{1,0:T(8,128)} %get-tuple-element.4) | copy-start | bytes 2457604
Sparse Core Ops, SparseCore 0:
  75.5 89.5 all-reduce.6
  168.9 104.4 all-reduce.4
